TPU v7x, 32 devices: a whole 2x2x4 slice. The times are simulated.
32 devices in a mesh: car: 2 (over y), branch: 4 (over x, core), pts: 4 (over z).
Axes of the slice: x: 2, y: 2, z: 4, core: 2. Of those that a mesh axis runs over, the one named last changes fastest.
Arguments:
- anchors: bfloat16 [512, 384], P(('car', 'branch', 'pts')), parts along dimension 0, may hold values from -6 to 6
- queries: bfloat16 [4096, 384], P(('car', 'branch', 'pts')), parts along dimension 0, may hold values from -6 to 6
- query_kind: int32 [4096], P(('car', 'branch', 'pts')), parts along dimension 0, may hold values from 0 to 1
- live_count: int32 [32], P(('car', 'branch', 'pts')), parts along dimension 0, may hold values from 16 to 128, as said below
- anchor_gain: float32 [384], replicated, may hold values from 0.25 to 1.75
- query_gain: float32 [384], replicated, may hold values from 0.25 to 1.75
- w_query: bfloat16 [384, 384], replicated, may hold values from -0.3125 to 0.3125
- w_key: bfloat16 [384, 384], replicated, may hold values from -0.3125 to 0.3125
- w_value: bfloat16 [384, 384], replicated, may hold values from -0.3125 to 0.3125
- w_out: bfloat16 [384, 384], replicated, may hold values from -0.3125 to 0.3125
- cotangent: bfloat16 [4096, 384], P(('car', 'branch', 'pts')), parts along dimension 0, may hold values from -6 to 6
Outputs:
- fields: bfloat16 [4096, 384], P(('car', 'branch', 'pts')), parts along dimension 0
- query_grad: float32 [4096, 384], P(('car', 'branch', 'pts')), parts along dimension 0
- anchor_grad: float32 [512, 384], P(('car', 'branch', 'pts')), parts along dimension 0
There are 2 independent parts, one for each index of `car`. A program takes and returns all parts, laid end to end along the dimension named above; an argument that names none is the same for every part. Nothing has to cross between parts.
Inputs may be any that keep to these rules, and one draw needn't show every extreme that they name: `live_count`: each entry counts used slots of one device's 128 slots, the used ones first; some device has all 128 used in every draw.
All inputs are finite; a program needn't handle non-finite values.
Results may differ from a plain program's by a relative error of at most 0.011.
Values may be sent and summed in bfloat16 or wider, within the bound.
No kernel may reach another device: no remote copies, remote signals or barrier semaphores. Data moves between devices by JAX's collectives and lax.ppermute only.
A program may use at most 64 MiB of HBM per device.

v0:
```python
import functools

import jax
import jax.numpy as jnp
from jax import lax
from jax.experimental import pallas as pl
from jax.experimental.pallas import tpu as pltpu
from jax.sharding import PartitionSpec as P


HEADS = 6
GROUP_AXES = ("branch", "pts")

NN = (((1,), (0,)), ((), ()))
NT = (((1,), (1,)), ((), ()))
TN = (((0,), (0,)), ((), ()))


def mm(a, b, dims):
    return lax.dot_general(a, b, dims, preferred_element_type=jnp.float32)


def centered(rows):
    values = rows.astype(jnp.float32)
    center = values - jnp.mean(values, axis=-1, keepdims=True)
    variance = jnp.mean(center * center, axis=-1, keepdims=True)
    return center, lax.rsqrt(variance + 1e-05)


def norm_pullback(center, scale, gain, grad):
    through = grad * gain
    inner = jnp.mean(through * center, axis=-1, keepdims=True)
    grad_center = scale * through - center * (scale * scale * scale * inner)
    return grad_center - jnp.mean(grad_center, axis=-1, keepdims=True)


def as_row(gain):
    return gain[...].reshape(1, -1)


def live_rows(count, rows):
    return (lax.broadcasted_iota(jnp.int32, (rows, 1), 0) < count).astype(jnp.float32)


def masked_pair(pair, head):
    first = lax.broadcasted_iota(jnp.int32, (1, 2 * head), 1) < head
    zero = jnp.zeros((), pair.dtype)
    return jnp.concatenate([jnp.where(first, pair, zero), jnp.where(first, zero, pair)], 0)


def put_pairs(out, rows, head):
    height = 2 * rows.shape[0]
    for k in range(rows.shape[1] // (2 * head)):
        out[k * height : (k + 1) * height, :] = masked_pair(rows[:, 2 * head * k : 2 * head * (k + 1)], head)


def query_side(queries, cot, gain, w_query, w_out, *refs):
    total = (len(refs) - 6) // 2
    sources, outs, count, sems = refs[: total + 1], refs[total + 1 : -2], refs[-2], refs[-1]
    (heads_out, grad_out, live_out), kept = outs[:3], outs[3:]
    copies = [pltpu.make_async_copy(a, b, sems.at[k]) for k, (a, b) in enumerate(zip(sources, kept + (count,)))]
    for copy in copies:
        copy.start()
    center, scale = centered(queries[...])
    query_normed = (center * scale * as_row(gain)).astype(jnp.bfloat16)
    width = queries.shape[1]
    heads = mm(query_normed, w_query[...], NN).astype(jnp.bfloat16)
    put_pairs(heads_out, heads * (1.0 / (width // HEADS) ** 0.5), width // HEADS)
    copies[total].wait()
    live = live_rows(count[0, 0], queries.shape[0])
    live_out[...] = live
    grad_rows = (cot[...].astype(jnp.float32) * live).astype(jnp.bfloat16)
    put_pairs(grad_out, mm(grad_rows, w_out[...], NT).astype(jnp.bfloat16), width // HEADS)
    for copy in copies[:total]:
        copy.wait()


def stage(*refs):
    total = len(refs) // 2
    copies = [pltpu.make_async_copy(refs[k], refs[total + k], refs[-1].at[k]) for k in range(total)]
    for copy in copies:
        copy.start()
    for copy in copies:
        copy.wait()


def pack(*refs):
    at = 0
    for ref in refs[:-1]:
        refs[-1][at : at + ref.shape[0], :] = ref[...]
        at += ref.shape[0]


def join(own, partner, gain, out, mine):
    size = own.shape[0]
    center, scale = centered(jnp.concatenate([own[...], partner[...]], 0))
    normed = (center * scale * as_row(gain)).astype(jnp.bfloat16)
    out[...] = normed
    mine[...] = normed[:size]


def fold(heads, grads, w_key, w_value, heads_back, grads_back):
    lanes = heads.shape[1]
    height = heads.shape[0] * lanes // w_key.shape[1]
    for rows, weight, out in ((heads, w_key, heads_back), (grads, w_value, grads_back)):
        for k in range(w_key.shape[1] // lanes):
            lines = slice(k * height, (k + 1) * height)
            product = mm(rows[lines, :], weight[:, k * lanes : (k + 1) * lanes], NT)
            out[lines, :] = product.astype(out.dtype)


def where_am_i():
    branch = lax.axis_index("branch")
    return branch % 2, (branch >= lax.axis_size("branch") // 2).astype(jnp.int32)


def ordered(first, second):
    core, _ = where_am_i()
    return jnp.where(core == 0, first, second), jnp.where(core == 0, second, first)


def attend(near, normed, kind, heads, grads, heads_back, grads_back, w_key, w_value, mixed_out, dq_out):
    keys = mm(normed, w_key[...], NN).astype(jnp.bfloat16)
    values = mm(normed, w_value[...], NN).astype(jnp.bfloat16)
    width = keys.shape[1]
    head = width // HEADS
    rows = kind.shape[1]
    score_scale = 1.0 / head**0.5
    _, volume = where_am_i()
    mine = (kind[...] == 1).astype(jnp.int32) == (volume if near else 1 - volume)
    mine = jnp.concatenate([mine.astype(jnp.int32)] * 2, 1) == 1

    def by_head(x):
        return jnp.concatenate([x[:, :rows], x[:, rows:]], 0)

    def span(k):
        return slice(2 * head * k, 2 * head * (k + 1))

    def lines(k):
        return slice(2 * rows * k, 2 * rows * (k + 1))

    def products(k):
        return mm(keys[:, span(k)], heads[lines(k), :], NT), mm(values[:, span(k)], grads[lines(k), :], NT)

    def soften(scores, grad_probs):
        expo = jnp.exp(scores - jnp.max(scores, axis=0, keepdims=True))
        total = jnp.sum(expo, axis=0, keepdims=True)
        probs = expo * jnp.where(mine, 1.0 / total, 0.0)
        delta = jnp.sum(grad_probs * probs, axis=0, keepdims=True)
        return probs.astype(jnp.bfloat16), (probs * (grad_probs - delta)).astype(jnp.bfloat16)

    pairs = range(width // (2 * head))
    raw = [products(k) for k in pairs]
    soft = [soften(*x) for x in raw]
    result = mm(jnp.concatenate([x[1] for x in soft], 1), heads_back[...], NN)
    result = result + mm(jnp.concatenate([x[0] for x in soft], 1), grads_back[...], NN)
    for k in pairs:
        mixed = mm(by_head(soft[k][0]), masked_pair(values[:, span(k)], head), TN)
        mixed_out[:, span(k)] = mixed.astype(jnp.bfloat16)
        dq = mm(by_head(soft[k][1]), masked_pair(keys[:, span(k)], head), TN)
        dq_out[:, span(k)] = (dq * score_scale).astype(jnp.bfloat16)
    return result


def near_side(counts, kind, heads, grads, heads_back, grads_back, w_key, w_value, chip, *refs):
    both, split, _ = counts
    (got, other), (own_out, send_out, keep_out, mixed_out, dq_out) = refs[:2], refs[2:]
    pair = chip.shape[0]
    size = pair // 2
    blocks = [chip[...], got[: both * pair, :], other[: both * pair, :]]
    for k in range(both, both + split):
        at = slice(k * pair, (k + 1) * pair)
        blocks.append(ordered(got[at, :], other[at, :])[0])
    grad = attend(True, jnp.concatenate(blocks, 0), kind, heads, grads, heads_back, grads_back, w_key, w_value, mixed_out, dq_out)
    middle = pair + both * pair
    own_out[...] = grad[:size]
    send_out[:size, :] = grad[size:pair].astype(jnp.bfloat16)
    send_out[size:, :] = grad[middle : middle + both * pair].astype(jnp.bfloat16)
    keep_out[: both * pair, :] = grad[pair:middle]
    keep_out[both * pair :, :] = grad[middle + both * pair :]


def far_side(counts, kind, heads, grads, heads_back, grads_back, w_key, w_value, got, other, got_far, other_far, kept, *refs):
    both, split, far = counts
    send_out, keep_out, mixed_out, dq_out = refs
    pair = got.shape[0] // (both + split)
    size = pair // 2
    span = far * pair + size
    blocks = [got_far[...], other_far[...]]
    for k in range(both, both + split):
        at = slice(k * pair, (k + 1) * pair)
        blocks.append(ordered(got[at, :], other[at, :])[1])
    grad = attend(False, jnp.concatenate(blocks, 0), kind, heads, grads, heads_back, grads_back, w_key, w_value, mixed_out, dq_out)
    keep_out[:span, :] = grad[:span]
    send_out[:span, :] = grad[span : 2 * span].astype(jnp.bfloat16)
    here, there = ordered(kept[both * pair :, :], grad[2 * span :])
    keep_out[span:, :] = here
    send_out[span:, :] = there.astype(jnp.bfloat16)


def field_rows(live, queries, near, far, w_out, fields):
    residual = queries[...].astype(jnp.float32) + mm(near[...] + far[...], w_out[...], NN)
    fields[...] = (live[...] * residual).astype(jnp.bfloat16)


def query_back(live, queries, cot, near, far, gain, w_query, query_grad):
    center, scale = centered(queries[...])
    back = norm_pullback(center, scale, as_row(gain), mm(near[...] + far[...], w_query[...], NT))
    query_grad[...] = live[...] * (cot[...].astype(jnp.float32) + back)


def add_near(own, keep, got, own_out, *sums):
    size = own.shape[0]
    pair = 2 * size
    own_out[...] = own[...] + got[:size, :].astype(jnp.float32)
    for k, out in enumerate(sums):
        at = k * pair
        out[...] = (keep[at : at + pair, :] + got[size + at : size + at + pair, :].astype(jnp.float32)).astype(out.dtype)


def add_far(keep, got, *sums):
    at = 0
    for out in sums:
        span = slice(at, at + out.shape[0])
        out[...] = (keep[span, :] + got[span, :].astype(jnp.float32)).astype(out.dtype)
        at += out.shape[0]


def add_chips(*refs):
    got, (own, own_out, send_out) = refs[:-3], refs[-3:]
    size = own.shape[0]
    total = got[0][...].astype(jnp.float32)
    for other in got[1:]:
        total = total + other[...].astype(jnp.float32)
    own_out[...] = own[...] + total[:size]
    send_out[...] = total[size:].astype(send_out.dtype)


def anchor_back(anchors, own, got, across, gain, out):
    center, scale = centered(anchors[...])
    grad = own[...] + got[...].astype(jnp.float32) + across[...].astype(jnp.float32)
    out[...] = norm_pullback(center, scale, as_row(gain), grad)


def call(body, outs, *args, staged=(), scratch=()):
    specs = [pl.BlockSpec(memory_space=pltpu.VMEM)] * len(args)
    placed = [pltpu.with_memory_space_constraint(x, pltpu.VMEM) for x in args]
    held = [x if x.size == 1 else pltpu.with_memory_space_constraint(x, pltpu.HBM) for x in staged]
    return pl.pallas_call(
        body,
        out_shape=[pltpu.VMEM(*out) if on_chip else jax.ShapeDtypeStruct(*out) for on_chip, *out in outs],
        in_specs=specs + [pl.BlockSpec(memory_space=pl.ANY if x.size == 1 else pltpu.HBM) for x in staged],
        out_specs=[pl.BlockSpec(memory_space=pltpu.VMEM)] * len(outs),
        scratch_shapes=list(scratch),
        compiler_params=pltpu.CompilerParams(vmem_limit_bytes=32 * 2**20),
    )(*placed, *held)


def exchange_plan(branches, pts):
    top = branches * pts // 2
    nears = [d for d in range(1, top) if not d & pts]
    fars = [d | top for d in nears]
    both = list(zip(nears[:-1:2], nears[1:-1:2]))
    far = list(zip(fars[:-1:2], fars[1:-1:2]))
    return both + [(nears[-1], fars[-1])] + far, (len(both), 1, len(far))


def on_device(sizes, anchors, queries, query_kind, live_count, anchor_gain, query_gain, w_query, w_key, w_value, w_out, cotangent):
    branches, pts = sizes
    group = branches * pts
    plan, counts = exchange_plan(branches, pts)
    both, split, far = counts
    early = both + split

    def send(x, deltas):
        return lax.ppermute(x, GROUP_AXES, [(i, i ^ deltas[(i // pts) % 2]) for i in range(group)])

    def swap(x):
        return send(x, (pts, pts))

    def cross(x):
        return send(x, (group // 2, group // 2))

    size, width = anchors.shape
    rows = queries.shape[0]
    pair = 2 * size
    f32, bf16 = jnp.float32, jnp.bfloat16
    stacked = (HEADS * rows, 2 * width // HEADS)
    partner = swap(anchors)
    needed = (anchors, anchor_gain, queries, cotangent, query_gain, w_query, w_out)
    local, anchor_gain, queries, cotangent, query_gain, w_query, w_out = call(
        stage,
        [(True, x.shape, x.dtype) for x in needed],
        staged=needed,
        scratch=[pltpu.SemaphoreType.DMA((len(needed),))],
    )
    chip, mine = call(join, [(True, (pair, width), bf16), (True, (size, width), bf16)], local, partner, anchor_gain)
    got = []
    for step in plan:
        got.append(send(chip, step))
    across = cross(mine)
    inputs = (w_key, w_value, query_kind.reshape(1, -1))
    heads, grads, live, w_key, w_value, query_kind = call(
        query_side,
        [(True, stacked, bf16)] * 2 + [(True, (rows, 1), f32)] + [(True, x.shape, x.dtype) for x in inputs],
        queries,
        cotangent,
        query_gain,
        w_query,
        w_out,
        staged=inputs + (live_count.reshape(1, 1),),
        scratch=[pltpu.SMEM((1, 1), jnp.int32), pltpu.SemaphoreType.DMA((len(inputs) + 1,))],
    )
    (got_near,) = call(pack, [(True, (pair * early, width), bf16)], *got[:early])
    other_near = swap(got_near)
    got_far = jnp.concatenate([across] + got[early:], 0)
    other_far = swap(got_far)
    folded = [(True, (HEADS * rows, width), bf16)] * 2
    heads_back, grads_back = call(fold, folded, heads, grads, w_key, w_value)
    common = (query_kind, heads, grads, heads_back, grads_back, w_key, w_value)
    rowwise = [(True, (rows, width), bf16)] * 2
    own, send_near, keep_near, mixed_near, dq_near = call(
        functools.partial(near_side, counts),
        [(True, (size, width), f32), (True, (size + pair * both, width), bf16), (True, (pair * early, width), f32)] + rowwise,
        *common,
        chip,
        got_near,
        other_near,
    )
    back_near = swap(send_near)
    send_far, keep_far, mixed_far, dq_far = call(
        functools.partial(far_side, counts),
        [(True, (size + pair * (far + split), width), bf16), (True, (size + pair * (far + split), width), f32)] + rowwise,
        *common,
        got_near,
        other_near,
        got_far,
        other_far,
        keep_near,
    )
    back_far = swap(send_far)
    own, *sums = call(
        add_near, [(True, (size, width), f32)] + [(True, (pair, width), bf16)] * both, own, keep_near, back_near
    )
    across, *more = call(
        add_far, [(True, (size, width), bf16)] + [(True, (pair, width), bf16)] * (far + split), keep_far, back_far
    )
    sums += more[far:] + more[:far]
    arrived = []
    for part, step in zip(sums, plan):
        arrived.append(send(part, step))
    across = cross(across)
    (fields,) = call(field_rows, [(False, (rows, width), bf16)], live, queries, mixed_near, mixed_far, w_out)
    (query_grad,) = call(
        query_back, [(False, (rows, width), f32)],
        live, queries, cotangent, dq_near, dq_far, query_gain, w_query,
    )
    own, last = call(add_chips, [(True, (size, width), f32), (True, (size, width), bf16)], *arrived, own)
    last = swap(last)
    (anchor_grad,) = call(anchor_back, [(True, (size, width), f32)], local, own, last, across, anchor_gain)
    return fields, query_grad, anchor_grad


def solution(mesh):
    split = P(("car",) + GROUP_AXES, None)
    flat = P(("car",) + GROUP_AXES)
    sizes = mesh.shape["branch"], mesh.shape["pts"]

    def body(*args):
        return on_device(sizes, *args)

    return jax.shard_map(
        body,
        mesh=mesh,
        in_specs=(split, split, flat, flat, P(), P(), P(), P(), P(), P(), split),
        out_specs=(split, split, split),
        check_vma=False,
    )
```

profile of v0, /device:TPU:0, one launch (start us, length us, event | category | flops | bytes accessed | tf_op | source)
XLA Modules:
  0.0 30.9 jit_solution(2491790481158674639)
XLA Ops:
  0.6 0.6 %collective-permute-start = (bf16[16,384]{1,0:T(8,128)(2,1)}, bf16[16,384]{1,0:T(8,128)(2,1)S(1)}, u32[]{:S(2)}, u32[]{:S(2)}) collective-permute-start(bf16[16,384]{1,0:T(8,128)(2,1)} %refs_0_.2), channel_id=1, source_target_pairs={{0,4},{1,5},{2,6},{3,7},{4,0},{5,1},{6,2},{7,3},{8,12},{9,13},{10,... | collective-permute-start | bytes 36872 | tf_op jit(solution)/shard_map/ppermute | solution.py:276
  1.2 1.3 %shard_map.130 = (bf16[16,384]{1,0:T(8,128)(2,1)S(1)}, f32[384]{0:T(512)S(1)}, bf16[128,384]{1,0:T(8,128)(2,1)S(1)}, bf16[128,384]{1,0:T(8,128)(2,1)S(1)}, f32[3...) custom-call(bf16[16,384]{1,0:T(8,128)(2,1)} %refs_0_.2, f32[384]{0:T(512)} %refs_1_.2, ...), custom_call_target="tpu_custom_call" | custom-call | tf_op jit(solution)/shard_map/pallas_call | solution.py:249
  2.5 0.2 shard_map.133
  2.6 2.7 %collective-permute-start.4 = (bf16[16,384]{1,0:T(8,128)(2,1)S(1)}, bf16[16,384]{1,0:T(8,128)(2,1)S(1)}, u32[]{:S(2)}, u32[]{:S(2)}) collective-permute-start(bf16[16,384]{1,0:T(8,128)(2,1)S(1)} %get-tuple-element.53), channel_id=1, source_target_pairs={{0,8},{1,9},{2,10},{3,11},{4,12},{5,13},{6,14},{7,15},{8,0},{9,1},... | collective-permute-start | bytes 36872 | tf_op jit(solution)/shard_map/ppermute | solution.py:276
  5.3 1.5 %collective-permute-start.5 = (bf16[32,384]{1,0:T(8,128)(2,1)S(1)}, bf16[32,384]{1,0:T(8,128)(2,1)S(1)}, u32[]{:S(2)}, u32[]{:S(2)}) collective-permute-start(bf16[32,384]{1,0:T(8,128)(2,1)S(1)} %get-tuple-element.51.chip), channel_id=1, source_target_pairs={{0,9},{1,8},{2,11},{3,10},{4,14},{5,15},{6,12},{7,13},{8,1},{9,0},... | collective-permute-start | bytes 73736 | tf_op jit(solution)/shard_map/ppermute | solution.py:276
  6.8 2.5 %collective-permute-start.2 = (bf16[32,384]{1,0:T(8,128)(2,1)S(1)}, bf16[32,384]{1,0:T(8,128)(2,1)S(1)}, u32[]{:S(2)}, u32[]{:S(2)}) collective-permute-start(bf16[32,384]{1,0:T(8,128)(2,1)S(1)} %get-tuple-element.51.chip), channel_id=1, source_target_pairs={{0,3},{1,2},{2,1},{3,0},{4,15},{5,14},{6,13},{7,12},{8,11},{9,10},... | collective-permute-start | bytes 73736 | tf_op jit(solution)/shard_map/ppermute | solution.py:276
  9.3 0.7 %collective-permute-start.1 = (bf16[32,384]{1,0:T(8,128)(2,1)S(1)}, bf16[32,384]{1,0:T(8,128)(2,1)S(1)}, u32[]{:S(2)}, u32[]{:S(2)}) collective-permute-start(bf16[32,384]{1,0:T(8,128)(2,1)S(1)} %get-tuple-element.51.chip), channel_id=1, source_target_pairs={{0,1},{1,0},{2,3},{3,2},{4,6},{5,7},{6,4},{7,5},{8,9},{9,8},{10,11... | collective-permute-start | bytes 73736 | tf_op jit(solution)/shard_map/ppermute | solution.py:276
  10.0 0.0 collective-permute-done.4
  10.0 2.5 %collective-permute-done.2.refs_1_ = bf16[32,384]{1,0:T(8,128)(2,1)S(1)} collective-permute-done((bf16[32,384]{1,0:T(8,128)(2,1)S(1)}, bf16[32,384]{1,0:T(8,128)(2,1)S(1)}, u32[]{:S(2)}, u32[]{:S(2)}) %collective-permute-start.2) | collective-permute-done | bytes 24608 | tf_op jit(solution)/shard_map/ppermute | solution.py:276
  12.5 0.9 %collective-permute-done.1.refs_0_ = bf16[32,384]{1,0:T(8,128)(2,1)S(1)} collective-permute-done((bf16[32,384]{1,0:T(8,128)(2,1)S(1)}, bf16[32,384]{1,0:T(8,128)(2,1)S(1)}, u32[]{:S(2)}, u32[]{:S(2)}) %collective-permute-start.1) | collective-permute-done | bytes 24608 | tf_op jit(solution)/shard_map/ppermute | solution.py:276
  13.4 0.2 collective-permute-start.3
  13.6 0.4 %collective-permute-start.6 = (bf16[48,384]{1,0:T(8,128)(2,1)S(1)}, bf16[48,384]{1,0:T(8,128)(2,1)S(1)}, u32[]{:S(2)}, u32[]{:S(2)}) collective-permute-start(bf16[48,384]{1,0:T(8,128)(2,1)S(1)} %constant_dynamic-update-slice_fusion.got_far), channel_id=1, source_target_pairs={{0,4},{1,5},{2,6},{3,7},{4,0},{5,1},{6,2},{7,3},{8,12},{9,13},{10,... | collective-permute-start | bytes 110600 | tf_op jit(solution)/shard_map/ppermute | solution.py:276
  14.7 1.1 %shard_map.131 = (bf16[768,128]{1,0:T(8,128)(2,1)S(1)}, bf16[768,128]{1,0:T(8,128)(2,1)S(1)}, f32[128,1]{1,0:T(8,128)S(1)}, bf16[384,384]{1,0:T(8,128)(2,1)S(1)}...) custom-call(bf16[128,384]{1,0:T(8,128)(2,1)S(1)} %get-tuple-element.36.queries, ...), custom_call_target="tpu_custom_call" | custom-call | tf_op jit(solution)/shard_map/pallas_call | solution.py:249
  15.8 0.5 %shard_map.132 = (bf16[768,384]{1,0:T(8,128)(2,1)S(1)}, bf16[768,384]{1,0:T(8,128)(2,1)S(1)}) custom-call(bf16[768,128]{1,0:T(8,128)(2,1)S(1)} %get-tuple-element.43.heads, bf16[768,128]{1,0:T(8,128)(2,1)S(1)} %get-tuple-element.44.grads, bf16[384,384]{1,0:T(8,128)(2,1)S(1)} %get-tuple-element.45.w_key, bf16[384,384]{1,0:T(8,128)(2,1)S(1)} %get-tuple-element.46.w_value), custom_call_target="tpu_custom_call" | custom-call | tf_op jit(solution)/shard_map/pallas_call | solution.py:249
  16.3 0.9 %shard_map.135 = (f32[16,384]{1,0:T(8,128)S(1)}, bf16[48,384]{1,0:T(8,128)(2,1)S(1)}, f32[64,384]{1,0:T(8,128)S(1)}, bf16[128,384]{1,0:T(8,128)(2,1)S(1)}, bf16[128,384]{1,0:T(8,128)(2,1)S(1)}) custom-call(s32[1,128]{1,0:T(1,128)S(1)} %get-tuple-element.42.kind, bf16[768,128]{1,0:T(8,128)(2,1)S(1)} %get-tuple-element.43.heads, ...), custom_call_target="tpu_custom_call" | custom-call | tf_op jit(solution)/shard_map/pallas_call | solution.py:249
  17.2 0.0 collective-permute-done.6.other_far
  17.2 0.9 %shard_map.136 = (bf16[80,384]{1,0:T(8,128)(2,1)S(1)}, f32[80,384]{1,0:T(8,128)S(1)}, bf16[128,384]{1,0:T(8,128)(2,1)S(1)}, bf16[128,384]{1,0:T(8,128)(2,1)S(1)}) custom-call(s32[1,128]{1,0:T(1,128)S(1)} %get-tuple-element.42.kind, bf16[768,128]{1,0:T(8,128)(2,1)S(1)} %get-tuple-element.43.heads, bf16[768,128]{1,0:T(8,128)(2,1)S(1)} %get-tuple-element.44.grads, ...), custom_call_target="tpu_custom_call" | custom-call | tf_op jit(solution)/shard_map/pallas_call | solution.py:249
  18.2 0.3 collective-permute-start.9
  18.4 0.3 %collective-permute-start.7 = (bf16[48,384]{1,0:T(8,128)(2,1)S(1)}, bf16[48,384]{1,0:T(8,128)(2,1)S(1)}, u32[]{:S(2)}, u32[]{:S(2)}) collective-permute-start(bf16[48,384]{1,0:T(8,128)(2,1)S(1)} %get-tuple-element.59), channel_id=1, source_target_pairs={{0,4},{1,5},{2,6},{3,7},{4,0},{5,1},{6,2},{7,3},{8,12},{9,13},{10,... | collective-permute-start | bytes 110600 | tf_op jit(solution)/shard_map/ppermute | solution.py:276
  18.7 0.9 %collective-permute-done.7.got = bf16[48,384]{1,0:T(8,128)(2,1)S(1)} collective-permute-done((bf16[48,384]{1,0:T(8,128)(2,1)S(1)}, bf16[48,384]{1,0:T(8,128)(2,1)S(1)}, u32[]{:S(2)}, u32[]{:S(2)}) %collective-permute-start.7) | collective-permute-done | bytes 36896 | tf_op jit(solution)/shard_map/ppermute | solution.py:276
  19.6 0.4 %collective-permute-start.8 = (bf16[32,384]{1,0:T(8,128)(2,1)S(1)}, bf16[32,384]{1,0:T(8,128)(2,1)S(1)}, u32[]{:S(2)}, u32[]{:S(2)}) collective-permute-start(bf16[32,384]{1,0:T(8,128)(2,1)S(1)} %get-tuple-element.60), channel_id=1, source_target_pairs={{0,1},{1,0},{2,3},{3,2},{4,6},{5,7},{6,4},{7,5},{8,9},{9,8},{10,11... | collective-permute-start | bytes 73736 | tf_op jit(solution)/shard_map/ppermute | solution.py:276
  20.1 2.6 %collective-permute-start.10 = (bf16[32,384]{1,0:T(8,128)(2,1)S(1)}, bf16[32,384]{1,0:T(8,128)(2,1)S(1)}, u32[]{:S(2)}, u32[]{:S(2)}) collective-permute-start(bf16[32,384]{1,0:T(8,128)(2,1)S(1)} %get-tuple-element.63), channel_id=1, source_target_pairs={{0,3},{1,2},{2,1},{3,0},{4,15},{5,14},{6,13},{7,12},{8,11},{9,10},... | collective-permute-start | bytes 73736 | tf_op jit(solution)/shard_map/ppermute | solution.py:276
  22.7 0.9 %collective-permute-start.11 = (bf16[32,384]{1,0:T(8,128)(2,1)S(1)}, bf16[32,384]{1,0:T(8,128)(2,1)S(1)}, u32[]{:S(2)}, u32[]{:S(2)}) collective-permute-start(bf16[32,384]{1,0:T(8,128)(2,1)S(1)} %get-tuple-element.64), channel_id=1, source_target_pairs={{0,9},{1,8},{2,11},{3,10},{4,14},{5,15},{6,12},{7,13},{8,1},{9,0},... | collective-permute-start | bytes 73736 | tf_op jit(solution)/shard_map/ppermute | solution.py:276
  23.6 1.2 %collective-permute-start.13 = (bf16[16,384]{1,0:T(8,128)(2,1)S(1)}, bf16[16,384]{1,0:T(8,128)(2,1)S(1)}, u32[]{:S(2)}, u32[]{:S(2)}) collective-permute-start(bf16[16,384]{1,0:T(8,128)(2,1)S(1)} %get-tuple-element.68), channel_id=1, source_target_pairs={{0,8},{1,9},{2,10},{3,11},{4,12},{5,13},{6,14},{7,15},{8,0},{9,1},... | collective-permute-start | bytes 36872 | tf_op jit(solution)/shard_map/ppermute | solution.py:276
  24.8 0.0 collective-permute-done.8.refs_0_
  24.8 1.2 %collective-permute-done.10.refs_1_ = bf16[32,384]{1,0:T(8,128)(2,1)S(1)} collective-permute-done((bf16[32,384]{1,0:T(8,128)(2,1)S(1)}, bf16[32,384]{1,0:T(8,128)(2,1)S(1)}, u32[]{:S(2)}, u32[]{:S(2)}) %collective-permute-start.10) | collective-permute-done | bytes 24608 | tf_op jit(solution)/shard_map/ppermute | solution.py:276
  26.0 1.5 %collective-permute-done.11.refs_2_ = bf16[32,384]{1,0:T(8,128)(2,1)S(1)} collective-permute-done((bf16[32,384]{1,0:T(8,128)(2,1)S(1)}, bf16[32,384]{1,0:T(8,128)(2,1)S(1)}, u32[]{:S(2)}, u32[]{:S(2)}) %collective-permute-start.11) | collective-permute-done | bytes 24608 | tf_op jit(solution)/shard_map/ppermute | solution.py:276
  27.5 0.5 %collective-permute-start.12 = (bf16[16,384]{1,0:T(8,128)(2,1)S(1)}, bf16[16,384]{1,0:T(8,128)(2,1)S(1)}, u32[]{:S(2)}, u32[]{:S(2)}) collective-permute-start(bf16[16,384]{1,0:T(8,128)(2,1)S(1)} %get-tuple-element.67), channel_id=1, source_target_pairs={{0,4},{1,5},{2,6},{3,7},{4,0},{5,1},{6,2},{7,3},{8,12},{9,13},{10,... | collective-permute-start | bytes 36872 | tf_op jit(solution)/shard_map/ppermute | solution.py:276
  28.1 1.1 %shard_map.138 = f32[128,384]{1,0:T(8,128)} custom-call(f32[128,1]{1,0:T(8,128)S(1)} %get-tuple-element.41.live, bf16[128,384]{1,0:T(8,128)(2,1)S(1)} %get-tuple-element.36.queries, bf16[128,384]{1,0:T(8,128)(2,1)S(1)} %get-tuple-element.37.cot, bf16[128,384]{1,0:T(8,128)(2,1)S(1)} %get-tuple-element.56.near, bf16[128,384]{1,0:T(8,128)(2,1)S(1)} %get-tuple-element.57.far, ...), custom_call_target="tpu_custom_call" | custom-call | tf_op jit(solution)/shard_map/pallas_call | solution.py:249
  29.2 0.9 %shard_map.137 = bf16[128,384]{1,0:T(8,128)(2,1)} custom-call(f32[128,1]{1,0:T(8,128)S(1)} %get-tuple-element.41.live, bf16[128,384]{1,0:T(8,128)(2,1)S(1)} %get-tuple-element.36.queries, bf16[128,384]{1,0:T(8,128)(2,1)S(1)} %get-tuple-element.52.near, bf16[128,384]{1,0:T(8,128)(2,1)S(1)} %get-tuple-element.55.far, bf16[384,384]{1,0:T(8,128)(2,1)S(1)} %get-tuple-element.40.w_out), custom_call_target="tpu_custom_call" | custom-call | tf_op jit(solution)/shard_map/pallas_call | solution.py:249
  30.0 0.3 shard_map.142
  30.3 0.6 %copy.15 = f32[16,384]{1,0:T(8,128)} copy(f32[16,384]{1,0:T(8,128)S(1)} %shard_map.142) | data formatting | bytes 49152
  (12 shorter events, 0.1 us)
Async XLA Ops:
  0.6 1.8 %collective-permute-start = (bf16[16,384]{1,0:T(8,128)(2,1)}, bf16[16,384]{1,0:T(8,128)(2,1)S(1)}, u32[]{:S(2)}, u32[]{:S(2)}) collective-permute-start(bf16[16,384]{1,0:T(8,128)(2,1)} %refs_0_.2), channel_id=1, source_target_pairs={{0,4},{1,5},{2,6},{3,7},{4,0},{5,1},{6,2},{7,3},{8,12},{9,13},{10,... | collective-permute-start | bytes 36872 | tf_op jit(solution)/shard_map/ppermute | solution.py:276
  2.6 7.4 %collective-permute-start.4 = (bf16[16,384]{1,0:T(8,128)(2,1)S(1)}, bf16[16,384]{1,0:T(8,128)(2,1)S(1)}, u32[]{:S(2)}, u32[]{:S(2)}) collective-permute-start(bf16[16,384]{1,0:T(8,128)(2,1)S(1)} %get-tuple-element.53), channel_id=1, source_target_pairs={{0,8},{1,9},{2,10},{3,11},{4,12},{5,13},{6,14},{7,15},{8,0},{9,1},... | collective-permute-start | bytes 36872 | tf_op jit(solution)/shard_map/ppermute | solution.py:276
  5.3 8.3 %collective-permute-start.5 = (bf16[32,384]{1,0:T(8,128)(2,1)S(1)}, bf16[32,384]{1,0:T(8,128)(2,1)S(1)}, u32[]{:S(2)}, u32[]{:S(2)}) collective-permute-start(bf16[32,384]{1,0:T(8,128)(2,1)S(1)} %get-tuple-element.51.chip), channel_id=1, source_target_pairs={{0,9},{1,8},{2,11},{3,10},{4,14},{5,15},{6,12},{7,13},{8,1},{9,0},... | collective-permute-start | bytes 73736 | tf_op jit(solution)/shard_map/ppermute | solution.py:276
  6.8 5.6 %collective-permute-start.2 = (bf16[32,384]{1,0:T(8,128)(2,1)S(1)}, bf16[32,384]{1,0:T(8,128)(2,1)S(1)}, u32[]{:S(2)}, u32[]{:S(2)}) collective-permute-start(bf16[32,384]{1,0:T(8,128)(2,1)S(1)} %get-tuple-element.51.chip), channel_id=1, source_target_pairs={{0,3},{1,2},{2,1},{3,0},{4,15},{5,14},{6,13},{7,12},{8,11},{9,10},... | collective-permute-start | bytes 73736 | tf_op jit(solution)/shard_map/ppermute | solution.py:276
  9.3 4.1 %collective-permute-start.1 = (bf16[32,384]{1,0:T(8,128)(2,1)S(1)}, bf16[32,384]{1,0:T(8,128)(2,1)S(1)}, u32[]{:S(2)}, u32[]{:S(2)}) collective-permute-start(bf16[32,384]{1,0:T(8,128)(2,1)S(1)} %get-tuple-element.51.chip), channel_id=1, source_target_pairs={{0,1},{1,0},{2,3},{3,2},{4,6},{5,7},{6,4},{7,5},{8,9},{9,8},{10,11... | collective-permute-start | bytes 73736 | tf_op jit(solution)/shard_map/ppermute | solution.py:276
  13.4 2.8 %collective-permute-start.3 = (bf16[64,384]{1,0:T(8,128)(2,1)S(1)}, bf16[64,384]{1,0:T(8,128)(2,1)S(1)}, u32[]{:S(2)}, u32[]{:S(2)}) collective-permute-start(bf16[64,384]{1,0:T(8,128)(2,1)S(1)} %shard_map.134.refs_0_.got), channel_id=1, source_target_pairs={{0,4},{1,5},{2,6},{3,7},{4,0},{5,1},{6,2},{7,3},{8,12},{9,13},{10,... | collective-permute-start | bytes 147464 | tf_op jit(solution)/shard_map/ppermute | solution.py:276
  13.6 3.6 %collective-permute-start.6 = (bf16[48,384]{1,0:T(8,128)(2,1)S(1)}, bf16[48,384]{1,0:T(8,128)(2,1)S(1)}, u32[]{:S(2)}, u32[]{:S(2)}) collective-permute-start(bf16[48,384]{1,0:T(8,128)(2,1)S(1)} %constant_dynamic-update-slice_fusion.got_far), channel_id=1, source_target_pairs={{0,4},{1,5},{2,6},{3,7},{4,0},{5,1},{6,2},{7,3},{8,12},{9,13},{10,... | collective-permute-start | bytes 110600 | tf_op jit(solution)/shard_map/ppermute | solution.py:276
  18.2 1.9 %collective-permute-start.9 = (bf16[80,384]{1,0:T(8,128)(2,1)S(1)}, bf16[80,384]{1,0:T(8,128)(2,1)S(1)}, u32[]{:S(2)}, u32[]{:S(2)}) collective-permute-start(bf16[80,384]{1,0:T(8,128)(2,1)S(1)} %get-tuple-element.62), channel_id=1, source_target_pairs={{0,4},{1,5},{2,6},{3,7},{4,0},{5,1},{6,2},{7,3},{8,12},{9,13},{10,... | collective-permute-start | bytes 184328 | tf_op jit(solution)/shard_map/ppermute | solution.py:276
  18.4 1.2 %collective-permute-start.7 = (bf16[48,384]{1,0:T(8,128)(2,1)S(1)}, bf16[48,384]{1,0:T(8,128)(2,1)S(1)}, u32[]{:S(2)}, u32[]{:S(2)}) collective-permute-start(bf16[48,384]{1,0:T(8,128)(2,1)S(1)} %get-tuple-element.59), channel_id=1, source_target_pairs={{0,4},{1,5},{2,6},{3,7},{4,0},{5,1},{6,2},{7,3},{8,12},{9,13},{10,... | collective-permute-start | bytes 110600 | tf_op jit(solution)/shard_map/ppermute | solution.py:276
  19.6 5.1 %collective-permute-start.8 = (bf16[32,384]{1,0:T(8,128)(2,1)S(1)}, bf16[32,384]{1,0:T(8,128)(2,1)S(1)}, u32[]{:S(2)}, u32[]{:S(2)}) collective-permute-start(bf16[32,384]{1,0:T(8,128)(2,1)S(1)} %get-tuple-element.60), channel_id=1, source_target_pairs={{0,1},{1,0},{2,3},{3,2},{4,6},{5,7},{6,4},{7,5},{8,9},{9,8},{10,11... | collective-permute-start | bytes 73736 | tf_op jit(solution)/shard_map/ppermute | solution.py:276
  20.1 5.9 %collective-permute-start.10 = (bf16[32,384]{1,0:T(8,128)(2,1)S(1)}, bf16[32,384]{1,0:T(8,128)(2,1)S(1)}, u32[]{:S(2)}, u32[]{:S(2)}) collective-permute-start(bf16[32,384]{1,0:T(8,128)(2,1)S(1)} %get-tuple-element.63), channel_id=1, source_target_pairs={{0,3},{1,2},{2,1},{3,0},{4,15},{5,14},{6,13},{7,12},{8,11},{9,10},... | collective-permute-start | bytes 73736 | tf_op jit(solution)/shard_map/ppermute | solution.py:276
  22.7 4.8 %collective-permute-start.11 = (bf16[32,384]{1,0:T(8,128)(2,1)S(1)}, bf16[32,384]{1,0:T(8,128)(2,1)S(1)}, u32[]{:S(2)}, u32[]{:S(2)}) collective-permute-start(bf16[32,384]{1,0:T(8,128)(2,1)S(1)} %get-tuple-element.64), channel_id=1, source_target_pairs={{0,9},{1,8},{2,11},{3,10},{4,14},{5,15},{6,12},{7,13},{8,1},{9,0},... | collective-permute-start | bytes 73736 | tf_op jit(solution)/shard_map/ppermute | solution.py:276
  23.6 6.5 %collective-permute-start.13 = (bf16[16,384]{1,0:T(8,128)(2,1)S(1)}, bf16[16,384]{1,0:T(8,128)(2,1)S(1)}, u32[]{:S(2)}, u32[]{:S(2)}) collective-permute-start(bf16[16,384]{1,0:T(8,128)(2,1)S(1)} %get-tuple-element.68), channel_id=1, source_target_pairs={{0,8},{1,9},{2,10},{3,11},{4,12},{5,13},{6,14},{7,15},{8,0},{9,1},... | collective-permute-start | bytes 36872 | tf_op jit(solution)/shard_map/ppermute | solution.py:276
  27.5 2.5 %collective-permute-start.12 = (bf16[16,384]{1,0:T(8,128)(2,1)S(1)}, bf16[16,384]{1,0:T(8,128)(2,1)S(1)}, u32[]{:S(2)}, u32[]{:S(2)}) collective-permute-start(bf16[16,384]{1,0:T(8,128)(2,1)S(1)} %get-tuple-element.67), channel_id=1, source_target_pairs={{0,4},{1,5},{2,6},{3,7},{4,0},{5,1},{6,2},{7,3},{8,12},{9,13},{10,... | collective-permute-start | bytes 36872 | tf_op jit(solution)/shard_map/ppermute | solution.py:276
where the time goes:
time: 31.2 us; the launch traced here: 30.9 us
  starting transfers between devices  14.7 us (47%)
  Pallas kernels  7.13 us (23%)
  waiting for transfers between devices  7.1 us (23%)
  between operations  1.37 us (4%)
  local copies, waits for them, and re-layouts  0.63 us (2%)
    ppermute x14, starting transfers between devices, send(): lax.ppermute(x, GROUP_AXES, [(i, i ^ deltas[i // pts % 2]) for i in range...  14.7 us
    pallas_call x13, Pallas kernels, call(): pl.pallas_call(body, out_shape=[pltpu.VMEM(*out) if on_chip else jax.Shap...  7.13 us
    ppermute x14, waiting for transfers between devices, send(): lax.ppermute(x, GROUP_AXES, [(i, i ^ deltas[i // pts % 2]) for i in range...  7.1 us
  transfers between devices with their start and end apart: 14, of which 5 were waited for; matrix products, arithmetic and copies ran while one was open for 0% of the time, Pallas kernels for 19%

commit v1 on v0

--- a/solution.py
+++ b/solution.py
@@ -119,19 +119,15 @@
     return jnp.where(core == 0, first, second), jnp.where(core == 0, second, first)
 
 
-def attend(near, normed, kind, heads, grads, heads_back, grads_back, w_key, w_value, mixed_out, dq_out):
+def attend(near, normed, kind, heads, grads, heads_back, grads_back, w_key, w_value, probs_out, values_out, scores_out, keys_out):
     keys = mm(normed, w_key[...], NN).astype(jnp.bfloat16)
     values = mm(normed, w_value[...], NN).astype(jnp.bfloat16)
     width = keys.shape[1]
     head = width // HEADS
     rows = kind.shape[1]
-    score_scale = 1.0 / head**0.5
     _, volume = where_am_i()
     mine = (kind[...] == 1).astype(jnp.int32) == (volume if near else 1 - volume)
     mine = jnp.concatenate([mine.astype(jnp.int32)] * 2, 1) == 1
-
-    def by_head(x):
-        return jnp.concatenate([x[:, :rows], x[:, rows:]], 0)
 
     def span(k):
         return slice(2 * head * k, 2 * head * (k + 1))
@@ -152,26 +148,32 @@
     pairs = range(width // (2 * head))
     raw = [products(k) for k in pairs]
     soft = [soften(*x) for x in raw]
-    result = mm(jnp.concatenate([x[1] for x in soft], 1), heads_back[...], NN)
-    result = result + mm(jnp.concatenate([x[0] for x in soft], 1), grads_back[...], NN)
-    for k in pairs:
-        mixed = mm(by_head(soft[k][0]), masked_pair(values[:, span(k)], head), TN)
-        mixed_out[:, span(k)] = mixed.astype(jnp.bfloat16)
-        dq = mm(by_head(soft[k][1]), masked_pair(keys[:, span(k)], head), TN)
-        dq_out[:, span(k)] = (dq * score_scale).astype(jnp.bfloat16)
-    return result
+    probs, grad_scores = (jnp.concatenate([x[k] for x in soft], 1) for k in (0, 1))
+    probs_out[...], values_out[...], scores_out[...], keys_out[...] = probs, values, grad_scores, keys
+    return mm(grad_scores, heads_back[...], NN) + mm(probs, grads_back[...], NN)
+
+
+def row_sums(soft, features):
+    width = features.shape[1]
+    head, rows = width // HEADS, soft.shape[1] // HEADS
+    parts = []
+    for k in range(width // (2 * head)):
+        x = soft[:, 2 * rows * k : 2 * rows * (k + 1)]
+        x = jnp.concatenate([x[:, :rows], x[:, rows:]], 0)
+        parts.append(mm(x, masked_pair(features[:, 2 * head * k : 2 * head * (k + 1)], head), TN))
+    return jnp.concatenate(parts, 1)
 
 
 def near_side(counts, kind, heads, grads, heads_back, grads_back, w_key, w_value, chip, *refs):
     both, split, _ = counts
-    (got, other), (own_out, send_out, keep_out, mixed_out, dq_out) = refs[:2], refs[2:]
+    (got, other), (own_out, send_out, keep_out, *row_outs) = refs[:2], refs[2:]
     pair = chip.shape[0]
     size = pair // 2
     blocks = [chip[...], got[: both * pair, :], other[: both * pair, :]]
     for k in range(both, both + split):
         at = slice(k * pair, (k + 1) * pair)
         blocks.append(ordered(got[at, :], other[at, :])[0])
-    grad = attend(True, jnp.concatenate(blocks, 0), kind, heads, grads, heads_back, grads_back, w_key, w_value, mixed_out, dq_out)
+    grad = attend(True, jnp.concatenate(blocks, 0), kind, heads, grads, heads_back, grads_back, w_key, w_value, *row_outs)
     middle = pair + both * pair
     own_out[...] = grad[:size]
     send_out[:size, :] = grad[size:pair].astype(jnp.bfloat16)
@@ -182,7 +184,7 @@
 
 def far_side(counts, kind, heads, grads, heads_back, grads_back, w_key, w_value, got, other, got_far, other_far, kept, *refs):
     both, split, far = counts
-    send_out, keep_out, mixed_out, dq_out = refs
+    send_out, keep_out, *row_outs = refs
     pair = got.shape[0] // (both + split)
     size = pair // 2
     span = far * pair + size
@@ -190,7 +192,7 @@
     for k in range(both, both + split):
         at = slice(k * pair, (k + 1) * pair)
         blocks.append(ordered(got[at, :], other[at, :])[1])
-    grad = attend(False, jnp.concatenate(blocks, 0), kind, heads, grads, heads_back, grads_back, w_key, w_value, mixed_out, dq_out)
+    grad = attend(False, jnp.concatenate(blocks, 0), kind, heads, grads, heads_back, grads_back, w_key, w_value, *row_outs)
     keep_out[:span, :] = grad[:span]
     send_out[:span, :] = grad[span : 2 * span].astype(jnp.bfloat16)
     here, there = ordered(kept[both * pair :, :], grad[2 * span :])
@@ -198,14 +200,17 @@
     send_out[span:, :] = there.astype(jnp.bfloat16)
 
 
-def field_rows(live, queries, near, far, w_out, fields):
-    residual = queries[...].astype(jnp.float32) + mm(near[...] + far[...], w_out[...], NN)
+def field_rows(live, queries, near, near_values, far, far_values, w_out, fields):
+    mixed = (row_sums(near, near_values) + row_sums(far, far_values)).astype(jnp.bfloat16)
+    residual = queries[...].astype(jnp.float32) + mm(mixed, w_out[...], NN)
     fields[...] = (live[...] * residual).astype(jnp.bfloat16)
 
 
-def query_back(live, queries, cot, near, far, gain, w_query, query_grad):
+def query_back(live, queries, cot, near, near_keys, far, far_keys, gain, w_query, query_grad):
+    score_scale = 1.0 / (queries.shape[1] // HEADS) ** 0.5
+    dq = ((row_sums(near, near_keys) + row_sums(far, far_keys)) * score_scale).astype(jnp.bfloat16)
     center, scale = centered(queries[...])
-    back = norm_pullback(center, scale, as_row(gain), mm(near[...] + far[...], w_query[...], NT))
+    back = norm_pullback(center, scale, as_row(gain), mm(dq, w_query[...], NT))
     query_grad[...] = live[...] * (cot[...].astype(jnp.float32) + back)
 
 
@@ -318,8 +323,9 @@
     folded = [(True, (HEADS * rows, width), bf16)] * 2
     heads_back, grads_back = call(fold, folded, heads, grads, w_key, w_value)
     common = (query_kind, heads, grads, heads_back, grads_back, w_key, w_value)
-    rowwise = [(True, (rows, width), bf16)] * 2
-    own, send_near, keep_near, mixed_near, dq_near = call(
+    half = group * size // 2
+    rowwise = [(True, (half, HEADS * rows), bf16), (True, (half, width), bf16)] * 2
+    own, send_near, keep_near, probs_near, values_near, scores_near, keys_near = call(
         functools.partial(near_side, counts),
         [(True, (size, width), f32), (True, (size + pair * both, width), bf16), (True, (pair * early, width), f32)] + rowwise,
         *common,
@@ -328,7 +334,7 @@
         other_near,
     )
     back_near = swap(send_near)
-    send_far, keep_far, mixed_far, dq_far = call(
+    send_far, keep_far, probs_far, values_far, scores_far, keys_far = call(
         functools.partial(far_side, counts),
         [(True, (size + pair * (far + split), width), bf16), (True, (size + pair * (far + split), width), f32)] + rowwise,
         *common,
@@ -350,10 +356,12 @@
     for part, step in zip(sums, plan):
         arrived.append(send(part, step))
     across = cross(across)
-    (fields,) = call(field_rows, [(False, (rows, width), bf16)], live, queries, mixed_near, mixed_far, w_out)
+    (fields,) = call(
+        field_rows, [(False, (rows, width), bf16)], live, queries, probs_near, values_near, probs_far, values_far, w_out
+    )
     (query_grad,) = call(
         query_back, [(False, (rows, width), f32)],
-        live, queries, cotangent, dq_near, dq_far, query_gain, w_query,
+        live, queries, cotangent, scores_near, keys_near, scores_far, keys_far, query_gain, w_query,
     )
     own, last = call(add_chips, [(True, (size, width), f32), (True, (size, width), bf16)], *arrived, own)
     last = swap(last)

time: 31.2 us -> 31.4 us (level)
  transfers between devices with their start and end apart: 14 -> 14, of which waited for: 5 -> 5; matrix products, arithmetic and copies ran while one was open for 0% -> 0% of each run, Pallas kernels for 19% -> 20%
where the time goes in v1:
time: 31.4 us; the launch traced here: 31.2 us
  starting transfers between devices  14.7 us (47%)
  Pallas kernels  7.42 us (24%)
  waiting for transfers between devices  7.1 us (23%)
  between operations  1.37 us (4%)
  local copies, waits for them, and re-layouts  0.63 us (2%)
    ppermute x14, starting transfers between devices, send(): lax.ppermute(x, GROUP_AXES, [(i, i ^ deltas[i // pts % 2]) for i in range...  14.7 us
    pallas_call x13, Pallas kernels, call(): pl.pallas_call(body, out_shape=[pltpu.VMEM(*out) if on_chip else jax.Shap...  7.42 us
    ppermute x14, waiting for transfers between devices, send(): lax.ppermute(x, GROUP_AXES, [(i, i ^ deltas[i // pts % 2]) for i in range...  7.1 us
  transfers between devices with their start and end apart: 14, of which 5 were waited for; matrix products, arithmetic and copies ran while one was open for 0% of the time, Pallas kernels for 20%

profile of v1, /device:TPU:0, one launch (start us, length us, event | category | flops | bytes accessed | tf_op | source)
XLA Modules:
  0.0 31.2 jit_solution(16971261130542436752)
XLA Ops:
  0.6 0.6 %collective-permute-start = (bf16[16,384]{1,0:T(8,128)(2,1)}, bf16[16,384]{1,0:T(8,128)(2,1)S(1)}, u32[]{:S(2)}, u32[]{:S(2)}) collective-permute-start(bf16[16,384]{1,0:T(8,128)(2,1)} %refs_0_.2), channel_id=1, source_target_pairs={{0,4},{1,5},{2,6},{3,7},{4,0},{5,1},{6,2},{7,3},{8,12},{9,13},{10,... | collective-permute-start | bytes 36872 | tf_op jit(solution)/shard_map/ppermute | solution.py:281
  1.2 1.3 %shard_map.130 = (bf16[16,384]{1,0:T(8,128)(2,1)S(1)}, f32[384]{0:T(512)S(1)}, bf16[128,384]{1,0:T(8,128)(2,1)S(1)}, bf16[128,384]{1,0:T(8,128)(2,1)S(1)}, f32[3...) custom-call(bf16[16,384]{1,0:T(8,128)(2,1)} %refs_0_.2, f32[384]{0:T(512)} %refs_1_.2, ...), custom_call_target="tpu_custom_call" | custom-call | tf_op jit(solution)/shard_map/pallas_call | solution.py:254
  2.5 0.2 shard_map.133
  2.6 2.7 %collective-permute-start.4 = (bf16[16,384]{1,0:T(8,128)(2,1)S(1)}, bf16[16,384]{1,0:T(8,128)(2,1)S(1)}, u32[]{:S(2)}, u32[]{:S(2)}) collective-permute-start(bf16[16,384]{1,0:T(8,128)(2,1)S(1)} %get-tuple-element.58), channel_id=1, source_target_pairs={{0,8},{1,9},{2,10},{3,11},{4,12},{5,13},{6,14},{7,15},{8,0},{9,1},... | collective-permute-start | bytes 36872 | tf_op jit(solution)/shard_map/ppermute | solution.py:281
  5.3 1.5 %collective-permute-start.5 = (bf16[32,384]{1,0:T(8,128)(2,1)S(1)}, bf16[32,384]{1,0:T(8,128)(2,1)S(1)}, u32[]{:S(2)}, u32[]{:S(2)}) collective-permute-start(bf16[32,384]{1,0:T(8,128)(2,1)S(1)} %get-tuple-element.55.chip), channel_id=1, source_target_pairs={{0,9},{1,8},{2,11},{3,10},{4,14},{5,15},{6,12},{7,13},{8,1},{9,0},... | collective-permute-start | bytes 73736 | tf_op jit(solution)/shard_map/ppermute | solution.py:281
  6.8 2.5 %collective-permute-start.2 = (bf16[32,384]{1,0:T(8,128)(2,1)S(1)}, bf16[32,384]{1,0:T(8,128)(2,1)S(1)}, u32[]{:S(2)}, u32[]{:S(2)}) collective-permute-start(bf16[32,384]{1,0:T(8,128)(2,1)S(1)} %get-tuple-element.55.chip), channel_id=1, source_target_pairs={{0,3},{1,2},{2,1},{3,0},{4,15},{5,14},{6,13},{7,12},{8,11},{9,10},... | collective-permute-start | bytes 73736 | tf_op jit(solution)/shard_map/ppermute | solution.py:281
  9.3 0.7 %collective-permute-start.1 = (bf16[32,384]{1,0:T(8,128)(2,1)S(1)}, bf16[32,384]{1,0:T(8,128)(2,1)S(1)}, u32[]{:S(2)}, u32[]{:S(2)}) collective-permute-start(bf16[32,384]{1,0:T(8,128)(2,1)S(1)} %get-tuple-element.55.chip), channel_id=1, source_target_pairs={{0,1},{1,0},{2,3},{3,2},{4,6},{5,7},{6,4},{7,5},{8,9},{9,8},{10,11... | collective-permute-start | bytes 73736 | tf_op jit(solution)/shard_map/ppermute | solution.py:281
  10.0 0.0 collective-permute-done.4
  10.0 2.5 %collective-permute-done.2.refs_1_ = bf16[32,384]{1,0:T(8,128)(2,1)S(1)} collective-permute-done((bf16[32,384]{1,0:T(8,128)(2,1)S(1)}, bf16[32,384]{1,0:T(8,128)(2,1)S(1)}, u32[]{:S(2)}, u32[]{:S(2)}) %collective-permute-start.2) | collective-permute-done | bytes 24608 | tf_op jit(solution)/shard_map/ppermute | solution.py:281
  12.5 0.9 %collective-permute-done.1.refs_0_ = bf16[32,384]{1,0:T(8,128)(2,1)S(1)} collective-permute-done((bf16[32,384]{1,0:T(8,128)(2,1)S(1)}, bf16[32,384]{1,0:T(8,128)(2,1)S(1)}, u32[]{:S(2)}, u32[]{:S(2)}) %collective-permute-start.1) | collective-permute-done | bytes 24608 | tf_op jit(solution)/shard_map/ppermute | solution.py:281
  13.4 0.2 collective-permute-start.3
  13.6 0.4 %collective-permute-start.6 = (bf16[48,384]{1,0:T(8,128)(2,1)S(1)}, bf16[48,384]{1,0:T(8,128)(2,1)S(1)}, u32[]{:S(2)}, u32[]{:S(2)}) collective-permute-start(bf16[48,384]{1,0:T(8,128)(2,1)S(1)} %constant_dynamic-update-slice_fusion.got_far), channel_id=1, source_target_pairs={{0,4},{1,5},{2,6},{3,7},{4,0},{5,1},{6,2},{7,3},{8,12},{9,13},{10,... | collective-permute-start | bytes 110600 | tf_op jit(solution)/shard_map/ppermute | solution.py:281
  14.7 1.1 %shard_map.131 = (bf16[768,128]{1,0:T(8,128)(2,1)S(1)}, bf16[768,128]{1,0:T(8,128)(2,1)S(1)}, f32[128,1]{1,0:T(8,128)S(1)}, bf16[384,384]{1,0:T(8,128)(2,1)S(1)}...) custom-call(bf16[128,384]{1,0:T(8,128)(2,1)S(1)} %get-tuple-element.40.queries, ...), custom_call_target="tpu_custom_call" | custom-call | tf_op jit(solution)/shard_map/pallas_call | solution.py:254
  15.8 0.5 %shard_map.132 = (bf16[768,384]{1,0:T(8,128)(2,1)S(1)}, bf16[768,384]{1,0:T(8,128)(2,1)S(1)}) custom-call(bf16[768,128]{1,0:T(8,128)(2,1)S(1)} %get-tuple-element.47.heads, bf16[768,128]{1,0:T(8,128)(2,1)S(1)} %get-tuple-element.48.grads, bf16[384,384]{1,0:T(8,128)(2,1)S(1)} %get-tuple-element.49.w_key, bf16[384,384]{1,0:T(8,128)(2,1)S(1)} %get-tuple-element.50.w_value), custom_call_target="tpu_custom_call" | custom-call | tf_op jit(solution)/shard_map/pallas_call | solution.py:254
  16.3 0.9 %shard_map.135 = (f32[16,384]{1,0:T(8,128)S(1)}, bf16[48,384]{1,0:T(8,128)(2,1)S(1)}, f32[64,384]{1,0:T(8,128)S(1)}, bf16[128,768]{1,0:T(8,128)(2,1)S(1)}, bf16[...) custom-call(s32[1,128]{1,0:T(1,128)S(1)} %get-tuple-element.46.kind, ...), custom_call_target="tpu_custom_call" | custom-call | tf_op jit(solution)/shard_map/pallas_call | solution.py:254
  17.1 0.0 collective-permute-done.6.other_far
  17.1 0.9 %shard_map.136 = (bf16[80,384]{1,0:T(8,128)(2,1)S(1)}, f32[80,384]{1,0:T(8,128)S(1)}, bf16[128,768]{1,0:T(8,128)(2,1)S(1)}, bf16[128,384]{1,0:T(8,128)(2,1)S(1)}...) custom-call(s32[1,128]{1,0:T(1,128)S(1)} %get-tuple-element.46.kind, ...), custom_call_target="tpu_custom_call" | custom-call | tf_op jit(solution)/shard_map/pallas_call | solution.py:254
  18.0 0.3 collective-permute-start.9
  18.3 0.3 %collective-permute-start.7 = (bf16[48,384]{1,0:T(8,128)(2,1)S(1)}, bf16[48,384]{1,0:T(8,128)(2,1)S(1)}, u32[]{:S(2)}, u32[]{:S(2)}) collective-permute-start(bf16[48,384]{1,0:T(8,128)(2,1)S(1)} %get-tuple-element.67), channel_id=1, source_target_pairs={{0,4},{1,5},{2,6},{3,7},{4,0},{5,1},{6,2},{7,3},{8,12},{9,13},{10,... | collective-permute-start | bytes 110600 | tf_op jit(solution)/shard_map/ppermute | solution.py:281
  18.6 0.9 %collective-permute-done.7.got = bf16[48,384]{1,0:T(8,128)(2,1)S(1)} collective-permute-done((bf16[48,384]{1,0:T(8,128)(2,1)S(1)}, bf16[48,384]{1,0:T(8,128)(2,1)S(1)}, u32[]{:S(2)}, u32[]{:S(2)}) %collective-permute-start.7) | collective-permute-done | bytes 36896 | tf_op jit(solution)/shard_map/ppermute | solution.py:281
  19.5 0.4 %collective-permute-start.8 = (bf16[32,384]{1,0:T(8,128)(2,1)S(1)}, bf16[32,384]{1,0:T(8,128)(2,1)S(1)}, u32[]{:S(2)}, u32[]{:S(2)}) collective-permute-start(bf16[32,384]{1,0:T(8,128)(2,1)S(1)} %get-tuple-element.68), channel_id=1, source_target_pairs={{0,1},{1,0},{2,3},{3,2},{4,6},{5,7},{6,4},{7,5},{8,9},{9,8},{10,11... | collective-permute-start | bytes 73736 | tf_op jit(solution)/shard_map/ppermute | solution.py:281
  19.9 0.0 collective-permute-done.9.got
  19.9 2.6 %collective-permute-start.10 = (bf16[32,384]{1,0:T(8,128)(2,1)S(1)}, bf16[32,384]{1,0:T(8,128)(2,1)S(1)}, u32[]{:S(2)}, u32[]{:S(2)}) collective-permute-start(bf16[32,384]{1,0:T(8,128)(2,1)S(1)} %get-tuple-element.71), channel_id=1, source_target_pairs={{0,3},{1,2},{2,1},{3,0},{4,15},{5,14},{6,13},{7,12},{8,11},{9,10},... | collective-permute-start | bytes 73736 | tf_op jit(solution)/shard_map/ppermute | solution.py:281
  22.5 0.9 %collective-permute-start.11 = (bf16[32,384]{1,0:T(8,128)(2,1)S(1)}, bf16[32,384]{1,0:T(8,128)(2,1)S(1)}, u32[]{:S(2)}, u32[]{:S(2)}) collective-permute-start(bf16[32,384]{1,0:T(8,128)(2,1)S(1)} %get-tuple-element.72), channel_id=1, source_target_pairs={{0,9},{1,8},{2,11},{3,10},{4,14},{5,15},{6,12},{7,13},{8,1},{9,0},... | collective-permute-start | bytes 73736 | tf_op jit(solution)/shard_map/ppermute | solution.py:281
  23.4 1.2 %collective-permute-start.13 = (bf16[16,384]{1,0:T(8,128)(2,1)S(1)}, bf16[16,384]{1,0:T(8,128)(2,1)S(1)}, u32[]{:S(2)}, u32[]{:S(2)}) collective-permute-start(bf16[16,384]{1,0:T(8,128)(2,1)S(1)} %get-tuple-element.76), channel_id=1, source_target_pairs={{0,8},{1,9},{2,10},{3,11},{4,12},{5,13},{6,14},{7,15},{8,0},{9,1},... | collective-permute-start | bytes 36872 | tf_op jit(solution)/shard_map/ppermute | solution.py:281
  24.6 1.2 %collective-permute-done.10.refs_1_ = bf16[32,384]{1,0:T(8,128)(2,1)S(1)} collective-permute-done((bf16[32,384]{1,0:T(8,128)(2,1)S(1)}, bf16[32,384]{1,0:T(8,128)(2,1)S(1)}, u32[]{:S(2)}, u32[]{:S(2)}) %collective-permute-start.10) | collective-permute-done | bytes 24608 | tf_op jit(solution)/shard_map/ppermute | solution.py:281
  25.9 1.5 %collective-permute-done.11.refs_2_ = bf16[32,384]{1,0:T(8,128)(2,1)S(1)} collective-permute-done((bf16[32,384]{1,0:T(8,128)(2,1)S(1)}, bf16[32,384]{1,0:T(8,128)(2,1)S(1)}, u32[]{:S(2)}, u32[]{:S(2)}) %collective-permute-start.11) | collective-permute-done | bytes 24608 | tf_op jit(solution)/shard_map/ppermute | solution.py:281
  27.4 0.5 %collective-permute-start.12 = (bf16[16,384]{1,0:T(8,128)(2,1)S(1)}, bf16[16,384]{1,0:T(8,128)(2,1)S(1)}, u32[]{:S(2)}, u32[]{:S(2)}) collective-permute-start(bf16[16,384]{1,0:T(8,128)(2,1)S(1)} %get-tuple-element.75), channel_id=1, source_target_pairs={{0,4},{1,5},{2,6},{3,7},{4,0},{5,1},{6,2},{7,3},{8,12},{9,13},{10,... | collective-permute-start | bytes 36872 | tf_op jit(solution)/shard_map/ppermute | solution.py:281
  27.9 1.3 %shard_map.138 = f32[128,384]{1,0:T(8,128)} custom-call(f32[128,1]{1,0:T(8,128)S(1)} %get-tuple-element.45.live, bf16[128,384]{1,0:T(8,128)(2,1)S(1)} %get-tuple-element.40.queries, bf16[128,384]{1,0:T(8,128)(2,1)S(1)} %get-tuple-element.41.cot, bf16[128,768]{1,0:T(8,128)(2,1)S(1)} %get-tuple-element.62.near, ...), custom_call_target="tpu_custom_call" | custom-call | tf_op jit(solution)/shard_map/pallas_call | solution.py:254
  29.2 1.1 %shard_map.137 = bf16[128,384]{1,0:T(8,128)(2,1)} custom-call(f32[128,1]{1,0:T(8,128)S(1)} %get-tuple-element.45.live, bf16[128,384]{1,0:T(8,128)(2,1)S(1)} %get-tuple-element.40.queries, bf16[128,768]{1,0:T(8,128)(2,1)S(1)} %get-tuple-element.56.near, bf16[128,384]{1,0:T(8,128)(2,1)S(1)} %get-tuple-element.57.near_values, ...), custom_call_target="tpu_custom_call" | custom-call | tf_op jit(solution)/shard_map/pallas_call | solution.py:254
  30.3 0.3 shard_map.142
  30.6 0.6 %copy.15 = f32[16,384]{1,0:T(8,128)} copy(f32[16,384]{1,0:T(8,128)S(1)} %shard_map.142) | data formatting | bytes 49152
  (12 shorter events, 0.1 us)
Async XLA Ops:
  0.6 1.8 %collective-permute-start = (bf16[16,384]{1,0:T(8,128)(2,1)}, bf16[16,384]{1,0:T(8,128)(2,1)S(1)}, u32[]{:S(2)}, u32[]{:S(2)}) collective-permute-start(bf16[16,384]{1,0:T(8,128)(2,1)} %refs_0_.2), channel_id=1, source_target_pairs={{0,4},{1,5},{2,6},{3,7},{4,0},{5,1},{6,2},{7,3},{8,12},{9,13},{10,... | collective-permute-start | bytes 36872 | tf_op jit(solution)/shard_map/ppermute | solution.py:281
  2.6 7.4 %collective-permute-start.4 = (bf16[16,384]{1,0:T(8,128)(2,1)S(1)}, bf16[16,384]{1,0:T(8,128)(2,1)S(1)}, u32[]{:S(2)}, u32[]{:S(2)}) collective-permute-start(bf16[16,384]{1,0:T(8,128)(2,1)S(1)} %get-tuple-element.58), channel_id=1, source_target_pairs={{0,8},{1,9},{2,10},{3,11},{4,12},{5,13},{6,14},{7,15},{8,0},{9,1},... | collective-permute-start | bytes 36872 | tf_op jit(solution)/shard_map/ppermute | solution.py:281
  5.3 8.3 %collective-permute-start.5 = (bf16[32,384]{1,0:T(8,128)(2,1)S(1)}, bf16[32,384]{1,0:T(8,128)(2,1)S(1)}, u32[]{:S(2)}, u32[]{:S(2)}) collective-permute-start(bf16[32,384]{1,0:T(8,128)(2,1)S(1)} %get-tuple-element.55.chip), channel_id=1, source_target_pairs={{0,9},{1,8},{2,11},{3,10},{4,14},{5,15},{6,12},{7,13},{8,1},{9,0},... | collective-permute-start | bytes 73736 | tf_op jit(solution)/shard_map/ppermute | solution.py:281
  6.8 5.6 %collective-permute-start.2 = (bf16[32,384]{1,0:T(8,128)(2,1)S(1)}, bf16[32,384]{1,0:T(8,128)(2,1)S(1)}, u32[]{:S(2)}, u32[]{:S(2)}) collective-permute-start(bf16[32,384]{1,0:T(8,128)(2,1)S(1)} %get-tuple-element.55.chip), channel_id=1, source_target_pairs={{0,3},{1,2},{2,1},{3,0},{4,15},{5,14},{6,13},{7,12},{8,11},{9,10},... | collective-permute-start | bytes 73736 | tf_op jit(solution)/shard_map/ppermute | solution.py:281
  9.3 4.1 %collective-permute-start.1 = (bf16[32,384]{1,0:T(8,128)(2,1)S(1)}, bf16[32,384]{1,0:T(8,128)(2,1)S(1)}, u32[]{:S(2)}, u32[]{:S(2)}) collective-permute-start(bf16[32,384]{1,0:T(8,128)(2,1)S(1)} %get-tuple-element.55.chip), channel_id=1, source_target_pairs={{0,1},{1,0},{2,3},{3,2},{4,6},{5,7},{6,4},{7,5},{8,9},{9,8},{10,11... | collective-permute-start | bytes 73736 | tf_op jit(solution)/shard_map/ppermute | solution.py:281
  13.4 2.8 %collective-permute-start.3 = (bf16[64,384]{1,0:T(8,128)(2,1)S(1)}, bf16[64,384]{1,0:T(8,128)(2,1)S(1)}, u32[]{:S(2)}, u32[]{:S(2)}) collective-permute-start(bf16[64,384]{1,0:T(8,128)(2,1)S(1)} %shard_map.134.refs_0_.got), channel_id=1, source_target_pairs={{0,4},{1,5},{2,6},{3,7},{4,0},{5,1},{6,2},{7,3},{8,12},{9,13},{10,... | collective-permute-start | bytes 147464 | tf_op jit(solution)/shard_map/ppermute | solution.py:281
  13.6 3.5 %collective-permute-start.6 = (bf16[48,384]{1,0:T(8,128)(2,1)S(1)}, bf16[48,384]{1,0:T(8,128)(2,1)S(1)}, u32[]{:S(2)}, u32[]{:S(2)}) collective-permute-start(bf16[48,384]{1,0:T(8,128)(2,1)S(1)} %constant_dynamic-update-slice_fusion.got_far), channel_id=1, source_target_pairs={{0,4},{1,5},{2,6},{3,7},{4,0},{5,1},{6,2},{7,3},{8,12},{9,13},{10,... | collective-permute-start | bytes 110600 | tf_op jit(solution)/shard_map/ppermute | solution.py:281
  18.0 1.9 %collective-permute-start.9 = (bf16[80,384]{1,0:T(8,128)(2,1)S(1)}, bf16[80,384]{1,0:T(8,128)(2,1)S(1)}, u32[]{:S(2)}, u32[]{:S(2)}) collective-permute-start(bf16[80,384]{1,0:T(8,128)(2,1)S(1)} %get-tuple-element.70), channel_id=1, source_target_pairs={{0,4},{1,5},{2,6},{3,7},{4,0},{5,1},{6,2},{7,3},{8,12},{9,13},{10,... | collective-permute-start | bytes 184328 | tf_op jit(solution)/shard_map/ppermute | solution.py:281
  18.3 1.2 %collective-permute-start.7 = (bf16[48,384]{1,0:T(8,128)(2,1)S(1)}, bf16[48,384]{1,0:T(8,128)(2,1)S(1)}, u32[]{:S(2)}, u32[]{:S(2)}) collective-permute-start(bf16[48,384]{1,0:T(8,128)(2,1)S(1)} %get-tuple-element.67), channel_id=1, source_target_pairs={{0,4},{1,5},{2,6},{3,7},{4,0},{5,1},{6,2},{7,3},{8,12},{9,13},{10,... | collective-permute-start | bytes 110600 | tf_op jit(solution)/shard_map/ppermute | solution.py:281
  19.5 5.1 %collective-permute-start.8 = (bf16[32,384]{1,0:T(8,128)(2,1)S(1)}, bf16[32,384]{1,0:T(8,128)(2,1)S(1)}, u32[]{:S(2)}, u32[]{:S(2)}) collective-permute-start(bf16[32,384]{1,0:T(8,128)(2,1)S(1)} %get-tuple-element.68), channel_id=1, source_target_pairs={{0,1},{1,0},{2,3},{3,2},{4,6},{5,7},{6,4},{7,5},{8,9},{9,8},{10,11... | collective-permute-start | bytes 73736 | tf_op jit(solution)/shard_map/ppermute | solution.py:281
  19.9 5.9 %collective-permute-start.10 = (bf16[32,384]{1,0:T(8,128)(2,1)S(1)}, bf16[32,384]{1,0:T(8,128)(2,1)S(1)}, u32[]{:S(2)}, u32[]{:S(2)}) collective-permute-start(bf16[32,384]{1,0:T(8,128)(2,1)S(1)} %get-tuple-element.71), channel_id=1, source_target_pairs={{0,3},{1,2},{2,1},{3,0},{4,15},{5,14},{6,13},{7,12},{8,11},{9,10},... | collective-permute-start | bytes 73736 | tf_op jit(solution)/shard_map/ppermute | solution.py:281
  22.5 4.8 %collective-permute-start.11 = (bf16[32,384]{1,0:T(8,128)(2,1)S(1)}, bf16[32,384]{1,0:T(8,128)(2,1)S(1)}, u32[]{:S(2)}, u32[]{:S(2)}) collective-permute-start(bf16[32,384]{1,0:T(8,128)(2,1)S(1)} %get-tuple-element.72), channel_id=1, source_target_pairs={{0,9},{1,8},{2,11},{3,10},{4,14},{5,15},{6,12},{7,13},{8,1},{9,0},... | collective-permute-start | bytes 73736 | tf_op jit(solution)/shard_map/ppermute | solution.py:281
  23.4 6.9 %collective-permute-start.13 = (bf16[16,384]{1,0:T(8,128)(2,1)S(1)}, bf16[16,384]{1,0:T(8,128)(2,1)S(1)}, u32[]{:S(2)}, u32[]{:S(2)}) collective-permute-start(bf16[16,384]{1,0:T(8,128)(2,1)S(1)} %get-tuple-element.76), channel_id=1, source_target_pairs={{0,8},{1,9},{2,10},{3,11},{4,12},{5,13},{6,14},{7,15},{8,0},{9,1},... | collective-permute-start | bytes 36872 | tf_op jit(solution)/shard_map/ppermute | solution.py:281
  27.4 3.0 %collective-permute-start.12 = (bf16[16,384]{1,0:T(8,128)(2,1)S(1)}, bf16[16,384]{1,0:T(8,128)(2,1)S(1)}, u32[]{:S(2)}, u32[]{:S(2)}) collective-permute-start(bf16[16,384]{1,0:T(8,128)(2,1)S(1)} %get-tuple-element.75), channel_id=1, source_target_pairs={{0,4},{1,5},{2,6},{3,7},{4,0},{5,1},{6,2},{7,3},{8,12},{9,13},{10,... | collective-permute-start | bytes 36872 | tf_op jit(solution)/shard_map/ppermute | solution.py:281
